TPU v7x, 32 devices: a whole 2x2x4 slice. The times are simulated.
32 devices in a mesh: groups: 2 (over y), freq: 16 (over z, x, core).
Axes of the slice: x: 2, y: 2, z: 4, core: 2. Of those that a mesh axis runs over, the one named last changes fastest.
Arguments:
- refl: bfloat16 [128, 2, 512, 512], P(('groups', 'freq')), parts along dimension 0, may hold values from -0.1875 to 0.1875
- refl_scale: float32 [128, 4], P(('groups', 'freq')), parts along dimension 0, may hold values from 0.5 to 4
- freq_index: int32 [128], P(('groups', 'freq')), parts along dimension 0, may hold values from 1 to 1023, as said below
- fd_plus: bfloat16 [4096, 32, 512], P(('groups', 'freq')), parts along dimension 0, may hold values from -6 to 6
- onset: int32 [32768], P(('groups', 'freq')), parts along dimension 0, may hold values from 128 to 767
Outputs:
- f_minus: bfloat16 [4096, 32, 512], P(('groups', 'freq')), parts along dimension 0
- f_plus: float32 [4096, 32, 512], P(('groups', 'freq')), parts along dimension 0
There are 2 independent parts, one for each index of `groups`. A program takes and returns all parts, laid end to end along the dimension named above; each array names one. Nothing has to cross between parts.
Inputs may be any that keep to these rules, and one draw needn't show every extreme that they name: `freq_index`: the bins are distinct and ascending; the first is 1 and the last is 1023.
All inputs are finite; a program needn't handle non-finite values.
Results may differ from a plain program's by a relative error of at most 0.01.
Values may be sent and summed in bfloat16 or wider, within the bound.
No kernel may reach another device: no remote copies, remote signals or barrier semaphores. Data moves between devices by JAX's collectives and lax.ppermute only.
A program may use at most 128 MiB of HBM per device.

v0:
```python
import math
import jax
import jax.numpy as jnp
from jax import lax
from jax.sharding import PartitionSpec as P


def to_columns(field):
    return lax.all_to_all(field, "freq", split_axis=1, concat_axis=0, tiled=True)


def to_time(field):
    return lax.all_to_all(field, "freq", split_axis=0, concat_axis=1, tiled=True)


def local(refl, refl_scale, freq_index, fd_plus, onset):
    nfreq_dev = refl.shape[0]
    nrec = refl.shape[2]
    t_dev, points, _ = fd_plus.shape
    columns = points * nrec
    nshard = lax.axis_size("freq")
    ntime = t_dev * nshard
    width = columns // nshard
    first_col = lax.axis_index("freq") * width
    bins, scales = (
        lax.all_gather(freq_index, "freq", axis=0, tiled=True),
        lax.all_gather(refl_scale, "freq", axis=0, tiled=True),
    )
    nblocks = scales.shape[1]
    times = jnp.arange(ntime, dtype=jnp.int32)
    phase = bins[:, None] * times[None, :] % ntime
    angle = phase.astype(jnp.float32) * jnp.float32(2.0 * math.pi / ntime)
    cosine = jnp.cos(angle).astype(jnp.bfloat16)
    sine = jnp.sin(angle).astype(jnp.bfloat16)
    col_ids = first_col + jnp.arange(width, dtype=jnp.int32)
    block_ids = col_ids % nrec // (nrec // nblocks)
    onehot = (block_ids[None, :] == jnp.arange(nblocks, dtype=jnp.int32)[:, None]).astype(
        jnp.float32
    )
    col_scale = jnp.dot(
        scales, onehot, precision=lax.Precision.HIGHEST, preferred_element_type=jnp.float32
    )
    signed = jnp.where(times < ntime // 2, times, times - ntime)
    keep = (jnp.abs(signed)[:, None] < onset[None, :]).astype(jnp.float32)
    contract_time = (((0,), (0,)), ((), ()))

    def forward(colfield, table_c, table_s):
        real = jnp.dot(table_c, colfield, preferred_element_type=jnp.float32)
        imag = -jnp.dot(table_s, colfield, preferred_element_type=jnp.float32)
        spectrum = jnp.stack(
            [(real * col_scale).astype(jnp.bfloat16), (imag * col_scale).astype(jnp.bfloat16)],
            axis=1,
        )
        return lax.all_to_all(spectrum, "freq", split_axis=0, concat_axis=2, tiled=True)

    def convolve(spectrum, sign):
        spectrum = spectrum.reshape(nfreq_dev, 2, points, nrec)
        spec_r = spectrum[:, 0]
        spec_i = spectrum[:, 1]
        resp_r = refl[:, 0]
        resp_i = refl[:, 1]

        def apply(resp, spec):
            return jnp.einsum("frs,fvs->fvr", resp, spec, preferred_element_type=jnp.float32)

        out_r = apply(resp_r, spec_r) - sign * apply(resp_i, spec_i)
        out_i = apply(resp_r, spec_i) + sign * apply(resp_i, spec_r)
        stacked = jnp.stack([out_r.astype(jnp.bfloat16), out_i.astype(jnp.bfloat16)], axis=1)
        return lax.all_to_all(
            stacked.reshape(nfreq_dev, 2, columns), "freq", split_axis=2, concat_axis=0, tiled=True
        )

    def inverse(spectrum):
        trace = lax.dot_general(
            cosine, spectrum[:, 0], contract_time, preferred_element_type=jnp.float32
        )
        trace = trace - lax.dot_general(
            sine, spectrum[:, 1], contract_time, preferred_element_type=jnp.float32
        )
        return (trace * jnp.float32(2.0 / ntime) * keep).astype(jnp.bfloat16)

    direct = fd_plus.reshape(t_dev, columns)
    minus_cols = inverse(convolve(forward(to_columns(direct), cosine, sine), 1.0))
    minus_time = to_time(minus_cols)
    update_cols = inverse(convolve(forward(minus_cols, cosine, sine), -1.0))
    plus_time = direct.astype(jnp.float32) + to_time(update_cols).astype(jnp.float32)
    return (minus_time.reshape(t_dev, points, nrec), plus_time.reshape(t_dev, points, nrec))


def solution(mesh):
    return jax.shard_map(
        local,
        mesh=mesh,
        in_specs=(
            P(("groups", "freq"), None, None, None),
            P(("groups", "freq"), None),
            P(("groups", "freq")),
            P(("groups", "freq"), None, None),
            P(("groups", "freq")),
        ),
        out_specs=(P(("groups", "freq"), None, None), P(("groups", "freq"), None, None)),
        check_vma=False,
    )
```

profile of v0, /device:TPU:11, one launch (start us, length us, event | category | flops | bytes accessed | tf_op | source)
XLA Modules:
  0.0 541.2 jit_solution(8030469073627968279)
XLA Ops:
  0.6 7.9 %copy.51 = bf16[128,32,512]{0,2,1:T(8,128)(2,1)} copy(bf16[128,32,512]{2,1,0:T(8,128)(2,1)} %param.8) | data formatting | bytes 8388608 | tf_op args[3]
  8.5 6.7 %all-to-all-start = ((bf16[128,16,1024]{0,2,1:T(8,128)(2,1)}), bf16[128,16,1024]{0,2,1:T(8,128)(2,1)}, u32[]{:S(2)}, u32[]{:S(2)}) async-start(bf16[128,16,1024]{0,2,1:T(8,128)(2,1)} %bitcast.126), calls=%async_computation | async-start | bytes 8388608 | tf_op jit(solution)/shard_map/all_to_all | solution.py:9
  15.2 0.6 dynamic-slice
  16.5 0.2 dynamic-update-slice
  16.7 88.9 %all-reduce = s32[64]{0:T(128)S(1)} all-reduce(s32[64]{0:T(128)S(1)} %dynamic-update-slice), channel_id=1, replica_groups=mesh['groups'=2,'freq'=16] {'freq'}, use_global_device_ids=true, to_apply=%add | all-reduce | flops 64 | bytes 512
  105.6 18.6 %all-gather = f32[16,4,4]{2,1,0:T(4,128)S(1)} all-gather(f32[1,4,4]{2,1,0:T(4,128)S(1)} %bitcast.140), channel_id=1, replica_groups=mesh['groups'=2,'freq'=16] {'freq'}, dimensions={0}, use_global_device_ids=true | all-gather | bytes 1088 | tf_op jit(solution)/shard_map/all_gather | solution.py:27
  124.2 0.2 convolution_bitcast_fusion
  124.5 6.4 %copy.52 = bf16[16,128,1024]{2,1,0:T(8,128)(2,1)} copy(bf16[16,128,1024]{1,2,0:T(8,128)(2,1)} %bitcast.2) | data formatting | bytes 8388608 | tf_op jit(solution)/shard_map/all_to_all | solution.py:9
  130.9 4.5 fusion.64
  135.4 2.5 fusion.65
  138.0 0.3 copy.53
  138.2 15.2 %all_to_all.114 = bf16[64,2,1024]{2,1,0:T(2,128)(2,1)S(1)} all-to-all(bf16[64,2,1024]{2,1,0:T(2,128)(2,1)S(1)} %copy.53), channel_id=1, replica_groups=mesh['groups'=2,'freq'=16] {'freq'}, dimensions={0} | all-to-all | bytes 524288 | tf_op jit(solution)/shard_map/all_to_all | solution.py:54
  153.4 0.1 copy.94
  153.6 0.1 reshape.82
  153.7 2.4 fusion.6
  156.2 2.3 fusion.8
  158.5 0.7 fusion.56
  159.2 0.1 stack.40
  159.3 2.3 fusion.59
  161.6 0.1 stack.39
  161.7 0.2 pad_maximum_fusion.1
  161.9 13.0 %copy.57 = bf16[4,2,16384]{0,1,2:T(2,128)(2,1)} copy(bf16[4,2,16384]{2,0,1:T(4,128)(2,1)S(1)} %pad_maximum_fusion.1) | data formatting | bytes 524288 | tf_op jit(solution)/shard_map/stack | solution.py:68
  174.9 16.8 %reshape.93 = bf16[16,2,4096]{2,1,0:T(2,128)(2,1)} reshape(bf16[16384,2,4]{2,1,0:T(2,128)(2,1)} %bitcast.122) | data formatting | bytes 524288
  191.7 6.1 %all-to-all-start.2 = ((bf16[16,2,4096]{2,1,0:T(2,128)(2,1)}), bf16[16,2,4096]{2,1,0:T(2,128)(2,1)S(1)}, u32[]{:S(2)}, u32[]{:S(2)}) async-start(bf16[16,2,4096]{2,1,0:T(2,128)(2,1)} %reshape.93), calls=%async_computation.2 | async-start | bytes 524288 | tf_op jit(solution)/shard_map/all_to_all | solution.py:69
  197.8 7.9 %all-to-all-done.2 = bf16[16,2,4096]{2,1,0:T(2,128)(2,1)S(1)} async-done(((bf16[16,2,4096]{2,1,0:T(2,128)(2,1)}), bf16[16,2,4096]{2,1,0:T(2,128)(2,1)S(1)}, u32[]{:S(2)}, u32[]{:S(2)}) %all-to-all-start.2) | async-done | bytes 262176 | tf_op jit(solution)/shard_map/all_to_all | solution.py:69
  205.7 19.0 %reshape.94 = bf16[16384,2,4]{2,1,0:T(2,128)(2,1)} reshape(bf16[16,2,4096]{2,1,0:T(2,128)(2,1)S(1)} %all-to-all-done.2) | data formatting | bytes 524288
  224.7 11.9 %copy.67 = bf16[4,2,16,1024]{3,2,1,0:T(8,128)(2,1)S(1)} copy(bf16[4,2,16,1024]{0,1,3,2:T(2,128)(2,1)} %bitcast.123) | data formatting | bytes 524288 | tf_op jit(solution)/shard_map/all_to_all | solution.py:69
  236.6 0.3 copy.59
  236.9 0.4 fusion.123
  237.3 3.1 fusion.73
  240.4 4.1 fusion
  244.5 2.5 fusion.62
  247.1 2.5 fusion.63
  249.6 0.3 copy.61
  249.9 13.0 %all_to_all.115 = bf16[64,2,1024]{2,1,0:T(2,128)(2,1)S(1)} all-to-all(bf16[64,2,1024]{2,1,0:T(2,128)(2,1)S(1)} %copy.61), channel_id=1, replica_groups=mesh['groups'=2,'freq'=16] {'freq'}, dimensions={0} | all-to-all | bytes 524288 | tf_op jit(solution)/shard_map/all_to_all | solution.py:54
  262.9 0.1 copy.93
  263.1 0.1 reshape.84
  263.2 2.5 fusion.41
  265.7 2.3 fusion.38
  268.0 0.0 copy-done.1
  268.0 0.7 fusion.50
  268.7 0.1 stack.46
  268.8 2.3 fusion.53
  271.1 0.1 stack.45
  271.2 0.2 pad_maximum_fusion.3
  271.4 13.0 %copy.63 = bf16[4,2,16384]{0,1,2:T(2,128)(2,1)} copy(bf16[4,2,16384]{2,0,1:T(4,128)(2,1)S(1)} %pad_maximum_fusion.3) | data formatting | bytes 524288 | tf_op jit(solution)/shard_map/stack | solution.py:68
  284.4 16.2 %reshape.95 = bf16[16,2,4096]{2,1,0:T(2,128)(2,1)S(1)} reshape(bf16[16384,2,4]{2,1,0:T(2,128)(2,1)} %bitcast.124) | data formatting | bytes 524288
  300.6 12.8 %all_to_all.116 = bf16[16,2,4096]{2,1,0:T(2,128)(2,1)S(1)} all-to-all(bf16[16,2,4096]{2,1,0:T(2,128)(2,1)S(1)} %reshape.95), channel_id=1, replica_groups=mesh['groups'=2,'freq'=16] {'freq'}, dimensions={0} | all-to-all | bytes 524288 | tf_op jit(solution)/shard_map/all_to_all | solution.py:69
  313.4 6.5 %all-to-all-start.3 = ((bf16[16,128,1024]{2,1,0:T(8,128)(2,1)}), bf16[16,128,1024]{2,1,0:T(8,128)(2,1)}, u32[]{:S(2)}, u32[]{:S(2)}) async-start(bf16[16,128,1024]{2,1,0:T(8,128)(2,1)} %bitcast.127), calls=%async_computation.3 | async-start | bytes 8388608 | tf_op jit(solution)/shard_map/all_to_all | solution.py:13
  319.9 19.1 %reshape.96 = bf16[16384,2,4]{2,1,0:T(2,128)(2,1)} reshape(bf16[16,2,4096]{2,1,0:T(2,128)(2,1)S(1)} %all_to_all.116) | data formatting | bytes 524288
  338.9 11.9 %copy.68 = bf16[4,2,16,1024]{3,2,1,0:T(8,128)(2,1)S(1)} copy(bf16[4,2,16,1024]{0,1,3,2:T(2,128)(2,1)} %bitcast.125) | data formatting | bytes 524288 | tf_op jit(solution)/shard_map/all_to_all | solution.py:69
  350.8 0.3 copy.65
  351.1 0.4 fusion.122
  351.5 3.1 fusion.72
  354.6 4.9 fusion.1
  359.5 52.8 %all-to-all-done.3 = bf16[16,128,1024]{2,1,0:T(8,128)(2,1)} async-done(((bf16[16,128,1024]{2,1,0:T(8,128)(2,1)}), bf16[16,128,1024]{2,1,0:T(8,128)(2,1)}, u32[]{:S(2)}, u32[]{:S(2)}) %all-to-all-start.3) | async-done | bytes 4194336 | tf_op jit(solution)/shard_map/all_to_all | solution.py:13
  412.4 5.2 all-to-all-start.6
  417.6 6.5 %copy.60 = bf16[128,16,1024]{2,1,0:T(8,128)(2,1)} copy(bf16[128,16,1024]{2,0,1:T(8,128)(2,1)} %bitcast.19) | data formatting | bytes 8388608 | tf_op jit(solution)/shard_map/all_to_all | solution.py:13
  424.1 7.1 %reshape.83 = bf16[128,32,512]{2,1,0:T(8,128)(2,1)} reshape(bf16[128,16,1024]{2,1,0:T(8,128)(2,1)} %copy.60) | data formatting | bytes 8388608 | tf_op jit(solution)/shard_map/reshape | solution.py:87
  431.2 78.7 %all-to-all-done.6 = bf16[16,128,1024]{2,1,0:T(8,128)(2,1)} async-done(((bf16[16,128,1024]{2,1,0:T(8,128)(2,1)}), bf16[16,128,1024]{2,1,0:T(8,128)(2,1)}, u32[]{:S(2)}, u32[]{:S(2)}) %all-to-all-start.6) | async-done | bytes 4194336 | tf_op jit(solution)/shard_map/all_to_all | solution.py:13
  509.9 3.2 convert_bitcast_fusion
  513.2 8.3 %copy.66 = f32[128,16,1024]{2,1,0:T(8,128)} copy(f32[128,16,1024]{2,0,1:T(8,128)S(1)} %convert_bitcast_fusion) | data formatting | bytes 16777216 | tf_op jit(solution)/shard_map/convert_element_type | solution.py:86
  521.4 9.3 %reshape.85 = f32[128,32,512]{2,1,0:T(8,128)} reshape(f32[128,16,1024]{2,1,0:T(8,128)} %copy.66) | data formatting | bytes 16777216 | tf_op jit(solution)/shard_map/convert_element_type | solution.py:86
  530.7 10.2 %convert_add_fusion = f32[128,32,512]{2,1,0:T(8,128)} fusion(f32[128,32,512]{2,1,0:T(8,128)} %reshape.85, bf16[128,32,512]{2,1,0:T(8,128)(2,1)} %param.8), kind=kLoop, calls=%fused_computation.5 | loop fusion | flops 4194304 | bytes 20971520 | tf_op jit(solution)/shard_map/add | solution.py:86
  (21 shorter events, 0.1 us)
Async XLA Ops:
  8.5 6.7 %copy-start.7 = (u32[32]{0:T(128)S(1)}, u32[32]{0:T(128)}, u32[]{:S(2)}) copy-start(u32[32]{0:T(128)} %constant.68) | copy-start | bytes 388
  8.5 8.0 %copy-start.6 = (s32[4]{0:T(128)S(1)}, s32[4]{0:T(128)}, u32[]{:S(2)}) copy-start(s32[4]{0:T(128)} %param.7) | copy-start | bytes 52
  8.5 97.1 %copy-start.4 = (f32[4,4]{1,0:T(4,128)S(1)}, f32[4,4]{1,0:T(4,128)}, u32[]{:S(2)}) copy-start(f32[4,4]{1,0:T(4,128)} %param.6) | copy-start | bytes 196
  8.5 115.9 %all-to-all-start = ((bf16[128,16,1024]{0,2,1:T(8,128)(2,1)}), bf16[128,16,1024]{0,2,1:T(8,128)(2,1)}, u32[]{:S(2)}, u32[]{:S(2)}) async-start(bf16[128,16,1024]{0,2,1:T(8,128)(2,1)} %bitcast.126), calls=%async_computation | async-start | bytes 8388608 | tf_op jit(solution)/shard_map/all_to_all | solution.py:9
  130.9 4.5 copy-start.3
  153.7 4.8 copy-start
  191.7 14.0 %all-to-all-start.2 = ((bf16[16,2,4096]{2,1,0:T(2,128)(2,1)}), bf16[16,2,4096]{2,1,0:T(2,128)(2,1)S(1)}, u32[]{:S(2)}, u32[]{:S(2)}) async-start(bf16[16,2,4096]{2,1,0:T(2,128)(2,1)} %reshape.93), calls=%async_computation.2 | async-start | bytes 524288 | tf_op jit(solution)/shard_map/all_to_all | solution.py:69
  237.3 3.1 copy-start.5
  244.5 5.1 copy-start.2
  263.2 4.8 copy-start.1
  313.4 99.0 %all-to-all-start.3 = ((bf16[16,128,1024]{2,1,0:T(8,128)(2,1)}), bf16[16,128,1024]{2,1,0:T(8,128)(2,1)}, u32[]{:S(2)}, u32[]{:S(2)}) async-start(bf16[16,128,1024]{2,1,0:T(8,128)(2,1)} %bitcast.127), calls=%async_computation.3 | async-start | bytes 8388608 | tf_op jit(solution)/shard_map/all_to_all | solution.py:13
  412.4 97.6 %all-to-all-start.6 = ((bf16[16,128,1024]{2,1,0:T(8,128)(2,1)}), bf16[16,128,1024]{2,1,0:T(8,128)(2,1)}, u32[]{:S(2)}, u32[]{:S(2)}) async-start(bf16[16,128,1024]{2,1,0:T(8,128)(2,1)} %bitcast.128), calls=%async_computation.6 | async-start | bytes 8388608 | tf_op jit(solution)/shard_map/all_to_all | solution.py:13
where the time goes:
time: 550 us; the launch traced here: 541 us
  local copies, waits for them, and re-layouts  170 us (31%)
  blocking collectives  149 us (27%)
  waiting for transfers between devices  139 us (25%)
  matrix products  43.1 us (8%)
  starting transfers between devices  24.6 us (4%)
  other arithmetic  13.8 us (3%)
    all_to_all x2, waiting for transfers between devices, to_time(): lax.all_to_all(field, 'freq', split_axis=0, concat_axis=1, tiled=True)  132 us
    unnamed x1, blocking collectives  88.9 us
    unnamed x24, local copies, waits for them, and re-layouts  79.9 us
    all_to_all x2, blocking collectives, forward(): lax.all_to_all(spectrum, 'freq', split_axis=0, concat_axis=2, tiled=True)  28.2 us
    another operation x6, local copies, waits for them, and re-layouts, convolve(): jnp.stack([out_r.astype(jnp.bfloat16), out_i.astype(jnp.bfloat16)], axis=1)  26.2 us
    all_to_all x4, local copies, waits for them, and re-layouts, convolve(): lax.all_to_all(stacked.reshape(nfreq_dev, 2, columns), 'freq', split_axis...  24.3 us
    all_gather x1, blocking collectives, local(): lax.all_gather(refl_scale, 'freq', axis=0, tiled=True)  18.6 us
    convert_element_type x2, local copies, waits for them, and re-layouts, local(): to_time(update_cols).astype(jnp.float32)  17.6 us
  transfers between devices with their start and end apart: 4, of which 3 were waited for; matrix products, arithmetic and copies ran while one was open for 10% of the time, Pallas kernels for 0%

commit v1 on v0

--- a/solution.py
+++ b/solution.py
@@ -1,8 +1,39 @@
+import functools
 import math
 import jax
 import jax.numpy as jnp
 from jax import lax
 from jax.sharding import PartitionSpec as P
+
+
+def _lead_lane(s0, dim_at):
+    s0 = jnp.moveaxis(s0, 0, dim_at)
+    extra = s0.shape
+    met_up = s0.reshape(*extra[:dim_at], extra[dim_at] * extra[dim_at + 1], *extra[dim_at + 2 :])
+    return met_up
+
+
+def supply_slot(page, peer_axis):
+    size_here = lax.psum(1, axis_name=peer_axis)
+    step_out = page[None]
+    for j in range(size_here.bit_length() - 1):
+        tmp = 1 << j
+        inbox = []
+        for k0 in range(size_here):
+            inbox.append((k0, k0 ^ tmp))
+        f_next = lax.ppermute(step_out, peer_axis, perm=inbox)
+        work_now = jnp.stack([step_out, f_next])
+        u_next = lax.axis_index(peer_axis) >> j & 1
+        step_out = jnp.where(u_next == 0, work_now, work_now[::-1]).reshape(-1, *page.shape)
+    return step_out
+
+
+def plan_files(xs, my_tile, dim_no):
+    x_next = _lead_lane(supply_slot(xs, my_tile), dim_no)
+    return x_next
+
+
+step_on_the_desk = functools.partial(plan_files, my_tile="freq", dim_no=0)
 
 
 def to_columns(field):
@@ -24,7 +55,7 @@
     first_col = lax.axis_index("freq") * width
     bins, scales = (
         lax.all_gather(freq_index, "freq", axis=0, tiled=True),
-        lax.all_gather(refl_scale, "freq", axis=0, tiled=True),
+        step_on_the_desk(refl_scale),
     )
     nblocks = scales.shape[1]
     times = jnp.arange(ntime, dtype=jnp.int32)

time: 550 us -> 533 us (0.969)
  blocking collectives: 149 us -> 59.2 us
  waiting for transfers between devices: 139 us -> 209 us
    unnamed x1, blocking collectives: 88.9 us -> 19.5 us
    ppermute x0 -> x4, waiting for transfers between devices: none -> 68.3 us  [supply_slot(): f_next = lax.ppermute(step_out, peer_axis, perm=inbox)]
    all_gather x1 -> x0, blocking collectives: 18.6 us -> none  [local(): lax.all_gather(refl_scale, 'freq', axis=0, tiled=True)]
  transfers between devices with their start and end apart: 4 -> 8, of which waited for: 3 -> 7; matrix products, arithmetic and copies ran while one was open for 10% -> 10% of each run, Pallas kernels for 0% -> 0%
where the time goes in v1:
time: 533 us; the launch traced here: 523 us
  waiting for transfers between devices  209 us (39%)
  local copies, waits for them, and re-layouts  170 us (32%)
  blocking collectives  59.2 us (11%)
  matrix products  43.2 us (8%)
  starting transfers between devices  25.8 us (5%)
  other arithmetic  13.9 us (3%)
    all_to_all x2, waiting for transfers between devices, to_time(): lax.all_to_all(field, 'freq', split_axis=0, concat_axis=1, tiled=True)  132 us
    unnamed x24, local copies, waits for them, and re-layouts  79.9 us
    ppermute x4, waiting for transfers between devices, supply_slot(): f_next = lax.ppermute(step_out, peer_axis, perm=inbox)  68.3 us
    all_to_all x2, blocking collectives, forward(): lax.all_to_all(spectrum, 'freq', split_axis=0, concat_axis=2, tiled=True)  26.9 us
    another operation x6, local copies, waits for them, and re-layouts, convolve(): jnp.stack([out_r.astype(jnp.bfloat16), out_i.astype(jnp.bfloat16)], axis=1)  26.2 us
    all_to_all x4, local copies, waits for them, and re-layouts, convolve(): lax.all_to_all(stacked.reshape(nfreq_dev, 2, columns), 'freq', split_axis...  24.3 us
    unnamed x1, blocking collectives  19.5 us
    convert_element_type x2, local copies, waits for them, and re-layouts, local(): to_time(update_cols).astype(jnp.float32)  17.6 us
  transfers between devices with their start and end apart: 8, of which 7 were waited for; matrix products, arithmetic and copies ran while one was open for 10% of the time, Pallas kernels for 0%

profile of v1, /device:TPU:11, one launch (start us, length us, event | category | flops | bytes accessed | tf_op | source)
XLA Modules:
  0.0 523.4 jit_solution(2789555168285376598)
XLA Ops:
  0.6 7.9 %copy.62 = bf16[128,32,512]{0,2,1:T(8,128)(2,1)} copy(bf16[128,32,512]{2,1,0:T(8,128)(2,1)} %param.8) | data formatting | bytes 8388608 | tf_op args[3]
  8.5 6.7 %all-to-all-start = ((bf16[128,16,1024]{0,2,1:T(8,128)(2,1)}), bf16[128,16,1024]{0,2,1:T(8,128)(2,1)}, u32[]{:S(2)}, u32[]{:S(2)}) async-start(bf16[128,16,1024]{0,2,1:T(8,128)(2,1)} %bitcast.140), calls=%async_computation | async-start | bytes 8388608 | tf_op jit(solution)/shard_map/all_to_all | solution.py:40
  15.2 0.4 collective-permute-start
  15.7 0.9 collective-permute-done
  16.6 0.3 collective-permute-start.1
  16.9 16.6 %collective-permute-done.1 = f32[2,4,4]{2,1,0:T(4,128)S(1)} collective-permute-done((f32[2,4,4]{2,1,0:T(4,128)S(1)}, f32[2,4,4]{2,1,0:T(4,128)S(1)}, u32[]{:S(2)}, u32[]{:S(2)}) %collective-permute-start.1) | collective-permute-done | bytes 160 | tf_op jit(solution)/shard_map/ppermute | solution.py:24
  33.5 0.4 collective-permute-start.2
  33.9 0.6 dynamic-slice
  34.5 50.8 %collective-permute-done.2 = f32[4,4,4]{2,1,0:T(4,128)S(1)} collective-permute-done((f32[4,4,4]{2,1,0:T(4,128)S(1)}, f32[4,4,4]{2,1,0:T(4,128)S(1)}, u32[]{:S(2)}, u32[]{:S(2)}) %collective-permute-start.2) | collective-permute-done | bytes 288 | tf_op jit(solution)/shard_map/ppermute | solution.py:24
  86.2 0.2 dynamic-update-slice
  86.4 19.5 %all-reduce = s32[64]{0:T(128)S(1)} all-reduce(s32[64]{0:T(128)S(1)} %dynamic-update-slice), channel_id=1, replica_groups=mesh['groups'=2,'freq'=16] {'freq'}, use_global_device_ids=true, to_apply=%add | all-reduce | flops 64 | bytes 512
  106.1 0.1 copy.66
  106.3 0.3 fusion.82
  106.6 1.5 all-to-all-done
  108.1 6.4 %copy.63 = bf16[16,128,1024]{2,1,0:T(8,128)(2,1)} copy(bf16[16,128,1024]{1,2,0:T(8,128)(2,1)} %bitcast.2) | data formatting | bytes 8388608 | tf_op jit(solution)/shard_map/all_to_all | solution.py:40
  114.5 4.5 fusion.64
  119.0 2.5 fusion.65
  121.6 0.3 copy.67
  121.9 13.8 %all_to_all.114 = bf16[64,2,1024]{2,1,0:T(2,128)(2,1)S(1)} all-to-all(bf16[64,2,1024]{2,1,0:T(2,128)(2,1)S(1)} %copy.67), channel_id=1, replica_groups=mesh['groups'=2,'freq'=16] {'freq'}, dimensions={0} | all-to-all | bytes 524288 | tf_op jit(solution)/shard_map/all_to_all | solution.py:85
  135.7 0.1 copy.110
  136.0 2.5 fusion.6
  138.4 2.3 fusion.8
  140.7 0.7 fusion.56
  141.6 2.3 fusion.59
  144.0 0.2 pad_maximum_fusion.1
  144.2 13.0 %copy.71 = bf16[4,2,16384]{0,1,2:T(2,128)(2,1)} copy(bf16[4,2,16384]{2,0,1:T(4,128)(2,1)S(1)} %pad_maximum_fusion.1) | data formatting | bytes 524288 | tf_op jit(solution)/shard_map/stack | solution.py:99
  157.1 16.8 %reshape.103 = bf16[16,2,4096]{2,1,0:T(2,128)(2,1)} reshape(bf16[16384,2,4]{2,1,0:T(2,128)(2,1)} %bitcast.136) | data formatting | bytes 524288
  173.9 6.1 %all-to-all-start.2 = ((bf16[16,2,4096]{2,1,0:T(2,128)(2,1)}), bf16[16,2,4096]{2,1,0:T(2,128)(2,1)S(1)}, u32[]{:S(2)}, u32[]{:S(2)}) async-start(bf16[16,2,4096]{2,1,0:T(2,128)(2,1)} %reshape.103), calls=%async_computation.2 | async-start | bytes 524288 | tf_op jit(solution)/shard_map/all_to_all | solution.py:100
  180.1 7.9 %all-to-all-done.2 = bf16[16,2,4096]{2,1,0:T(2,128)(2,1)S(1)} async-done(((bf16[16,2,4096]{2,1,0:T(2,128)(2,1)}), bf16[16,2,4096]{2,1,0:T(2,128)(2,1)S(1)}, u32[]{:S(2)}, u32[]{:S(2)}) %all-to-all-start.2) | async-done | bytes 262176 | tf_op jit(solution)/shard_map/all_to_all | solution.py:100
  187.9 19.0 %reshape.104 = bf16[16384,2,4]{2,1,0:T(2,128)(2,1)} reshape(bf16[16,2,4096]{2,1,0:T(2,128)(2,1)S(1)} %all-to-all-done.2) | data formatting | bytes 524288
  207.0 11.9 %copy.83 = bf16[4,2,16,1024]{3,2,1,0:T(8,128)(2,1)S(1)} copy(bf16[4,2,16,1024]{0,1,3,2:T(2,128)(2,1)} %bitcast.137) | data formatting | bytes 524288 | tf_op jit(solution)/shard_map/all_to_all | solution.py:100
  218.9 0.3 copy.73
  219.1 0.4 fusion.126
  219.5 3.1 fusion.73
  222.7 4.1 fusion
  226.8 2.5 fusion.62
  229.3 2.5 fusion.63
  231.9 0.3 copy.75
  232.2 13.0 %all_to_all.115 = bf16[64,2,1024]{2,1,0:T(2,128)(2,1)S(1)} all-to-all(bf16[64,2,1024]{2,1,0:T(2,128)(2,1)S(1)} %copy.75), channel_id=1, replica_groups=mesh['groups'=2,'freq'=16] {'freq'}, dimensions={0} | all-to-all | bytes 524288 | tf_op jit(solution)/shard_map/all_to_all | solution.py:85
  245.2 0.1 copy.109
  245.5 2.5 fusion.41
  247.9 2.3 fusion.38
  250.2 0.7 fusion.50
  251.1 2.3 fusion.53
  253.5 0.2 pad_maximum_fusion.3
  253.7 13.0 %copy.77 = bf16[4,2,16384]{0,1,2:T(2,128)(2,1)} copy(bf16[4,2,16384]{2,0,1:T(4,128)(2,1)S(1)} %pad_maximum_fusion.3) | data formatting | bytes 524288 | tf_op jit(solution)/shard_map/stack | solution.py:99
  266.6 16.2 %reshape.105 = bf16[16,2,4096]{2,1,0:T(2,128)(2,1)S(1)} reshape(bf16[16384,2,4]{2,1,0:T(2,128)(2,1)} %bitcast.138) | data formatting | bytes 524288
  282.8 12.8 %all_to_all.116 = bf16[16,2,4096]{2,1,0:T(2,128)(2,1)S(1)} all-to-all(bf16[16,2,4096]{2,1,0:T(2,128)(2,1)S(1)} %reshape.105), channel_id=1, replica_groups=mesh['groups'=2,'freq'=16] {'freq'}, dimensions={0} | all-to-all | bytes 524288 | tf_op jit(solution)/shard_map/all_to_all | solution.py:100
  295.6 6.5 %all-to-all-start.3 = ((bf16[16,128,1024]{2,1,0:T(8,128)(2,1)}), bf16[16,128,1024]{2,1,0:T(8,128)(2,1)}, u32[]{:S(2)}, u32[]{:S(2)}) async-start(bf16[16,128,1024]{2,1,0:T(8,128)(2,1)} %bitcast.141), calls=%async_computation.3 | async-start | bytes 8388608 | tf_op jit(solution)/shard_map/all_to_all | solution.py:44
  302.1 19.1 %reshape.106 = bf16[16384,2,4]{2,1,0:T(2,128)(2,1)} reshape(bf16[16,2,4096]{2,1,0:T(2,128)(2,1)S(1)} %all_to_all.116) | data formatting | bytes 524288
  321.2 11.9 %copy.84 = bf16[4,2,16,1024]{3,2,1,0:T(8,128)(2,1)S(1)} copy(bf16[4,2,16,1024]{0,1,3,2:T(2,128)(2,1)} %bitcast.139) | data formatting | bytes 524288 | tf_op jit(solution)/shard_map/all_to_all | solution.py:100
  333.1 0.3 copy.79
  333.4 0.4 fusion.125
  333.7 3.1 fusion.72
  336.9 4.9 fusion.1
  341.8 52.8 %all-to-all-done.3 = bf16[16,128,1024]{2,1,0:T(8,128)(2,1)} async-done(((bf16[16,128,1024]{2,1,0:T(8,128)(2,1)}), bf16[16,128,1024]{2,1,0:T(8,128)(2,1)}, u32[]{:S(2)}, u32[]{:S(2)}) %all-to-all-start.3) | async-done | bytes 4194336 | tf_op jit(solution)/shard_map/all_to_all | solution.py:44
  394.6 5.2 %all-to-all-start.6 = ((bf16[16,128,1024]{2,1,0:T(8,128)(2,1)}), bf16[16,128,1024]{2,1,0:T(8,128)(2,1)}, u32[]{:S(2)}, u32[]{:S(2)}) async-start(bf16[16,128,1024]{2,1,0:T(8,128)(2,1)} %bitcast.142), calls=%async_computation.6 | async-start | bytes 8388608 | tf_op jit(solution)/shard_map/all_to_all | solution.py:44
  399.8 6.5 %copy.74 = bf16[128,16,1024]{2,1,0:T(8,128)(2,1)} copy(bf16[128,16,1024]{2,0,1:T(8,128)(2,1)} %bitcast.28) | data formatting | bytes 8388608 | tf_op jit(solution)/shard_map/all_to_all | solution.py:44
  406.4 7.1 %reshape.95 = bf16[128,32,512]{2,1,0:T(8,128)(2,1)} reshape(bf16[128,16,1024]{2,1,0:T(8,128)(2,1)} %copy.74) | data formatting | bytes 8388608 | tf_op jit(solution)/shard_map/reshape | solution.py:118
  413.4 78.7 %all-to-all-done.6 = bf16[16,128,1024]{2,1,0:T(8,128)(2,1)} async-done(((bf16[16,128,1024]{2,1,0:T(8,128)(2,1)}), bf16[16,128,1024]{2,1,0:T(8,128)(2,1)}, u32[]{:S(2)}, u32[]{:S(2)}) %all-to-all-start.6) | async-done | bytes 4194336 | tf_op jit(solution)/shard_map/all_to_all | solution.py:44
  492.2 3.2 convert_bitcast_fusion
  495.4 8.3 %copy.80 = f32[128,16,1024]{2,1,0:T(8,128)} copy(f32[128,16,1024]{2,0,1:T(8,128)S(1)} %convert_bitcast_fusion) | data formatting | bytes 16777216 | tf_op jit(solution)/shard_map/convert_element_type | solution.py:117
  503.6 9.4 %reshape.97 = f32[128,32,512]{2,1,0:T(8,128)} reshape(f32[128,16,1024]{2,1,0:T(8,128)} %copy.80) | data formatting | bytes 16777216 | tf_op jit(solution)/shard_map/convert_element_type | solution.py:117
  513.0 10.2 %convert_add_fusion = f32[128,32,512]{2,1,0:T(8,128)} fusion(f32[128,32,512]{2,1,0:T(8,128)} %reshape.97, bf16[128,32,512]{2,1,0:T(8,128)(2,1)} %param.8), kind=kLoop, calls=%fused_computation.5 | loop fusion | flops 4194304 | bytes 20971520 | tf_op jit(solution)/shard_map/add | solution.py:117
  (40 shorter events, 1.1 us)
Async XLA Ops:
  8.5 6.7 %copy-start.4 = (f32[4,4]{1,0:T(4,128)S(1)}, f32[4,4]{1,0:T(4,128)}, u32[]{:S(2)}) copy-start(f32[4,4]{1,0:T(4,128)} %param.6) | copy-start | bytes 196
  8.5 25.4 %copy-start.7 = (u32[32]{0:T(128)S(1)}, u32[32]{0:T(128)}, u32[]{:S(2)}) copy-start(u32[32]{0:T(128)} %constant.74) | copy-start | bytes 388
  8.5 77.7 %copy-start.6 = (s32[4]{0:T(128)S(1)}, s32[4]{0:T(128)}, u32[]{:S(2)}) copy-start(s32[4]{0:T(128)} %param.7) | copy-start | bytes 52
  8.5 99.6 %all-to-all-start = ((bf16[128,16,1024]{0,2,1:T(8,128)(2,1)}), bf16[128,16,1024]{0,2,1:T(8,128)(2,1)}, u32[]{:S(2)}, u32[]{:S(2)}) async-start(bf16[128,16,1024]{0,2,1:T(8,128)(2,1)} %bitcast.140), calls=%async_computation | async-start | bytes 8388608 | tf_op jit(solution)/shard_map/all_to_all | solution.py:40
  15.2 1.4 collective-permute-start
  16.6 16.9 %collective-permute-start.1 = (f32[2,4,4]{2,1,0:T(4,128)S(1)}, f32[2,4,4]{2,1,0:T(4,128)S(1)}, u32[]{:S(2)}, u32[]{:S(2)}) collective-permute-start(f32[2,4,4]{2,1,0:T(4,128)S(1)} %get-tuple-element.7), channel_id=1, source_target_pairs={{0,2},{1,3},{2,0},{3,1},{4,6},{5,7},{6,4},{7,5},{8,10},{9,11},{10,... | collective-permute-start | bytes 392 | tf_op jit(solution)/shard_map/ppermute | solution.py:24
  33.5 51.8 %collective-permute-start.2 = (f32[4,4,4]{2,1,0:T(4,128)S(1)}, f32[4,4,4]{2,1,0:T(4,128)S(1)}, u32[]{:S(2)}, u32[]{:S(2)}) collective-permute-start(f32[4,4,4]{2,1,0:T(4,128)S(1)} %bitcast.155), channel_id=1, source_target_pairs={{0,4},{1,5},{2,6},{3,7},{4,0},{5,1},{6,2},{7,3},{8,12},{9,13},{10,... | collective-permute-start | bytes 776 | tf_op jit(solution)/shard_map/ppermute | solution.py:24
  85.4 20.6 %collective-permute-start.3 = (f32[8,4,4]{0,2,1:T(4,128)S(1)}, f32[8,4,4]{0,2,1:T(4,128)S(1)}, u32[]{:S(2)}, u32[]{:S(2)}) collective-permute-start(f32[8,4,4]{0,2,1:T(4,128)S(1)} %copy.82), channel_id=1, source_target_pairs={{0,8},{1,9},{2,10},{3,11},{4,12},{5,13},{6,14},{7,15},{8,0},{9,1},... | collective-permute-start | bytes 1544 | tf_op jit(solution)/shard_map/ppermute | solution.py:24
  114.5 4.5 copy-start.3
  136.0 4.8 copy-start
  173.9 14.0 %all-to-all-start.2 = ((bf16[16,2,4096]{2,1,0:T(2,128)(2,1)}), bf16[16,2,4096]{2,1,0:T(2,128)(2,1)S(1)}, u32[]{:S(2)}, u32[]{:S(2)}) async-start(bf16[16,2,4096]{2,1,0:T(2,128)(2,1)} %reshape.103), calls=%async_computation.2 | async-start | bytes 524288 | tf_op jit(solution)/shard_map/all_to_all | solution.py:100
  219.5 3.1 copy-start.5
  226.8 5.1 copy-start.2
  245.4 4.8 copy-start.1
  295.6 99.0 %all-to-all-start.3 = ((bf16[16,128,1024]{2,1,0:T(8,128)(2,1)}), bf16[16,128,1024]{2,1,0:T(8,128)(2,1)}, u32[]{:S(2)}, u32[]{:S(2)}) async-start(bf16[16,128,1024]{2,1,0:T(8,128)(2,1)} %bitcast.141), calls=%async_computation.3 | async-start | bytes 8388608 | tf_op jit(solution)/shard_map/all_to_all | solution.py:44
  394.6 97.6 %all-to-all-start.6 = ((bf16[16,128,1024]{2,1,0:T(8,128)(2,1)}), bf16[16,128,1024]{2,1,0:T(8,128)(2,1)}, u32[]{:S(2)}, u32[]{:S(2)}) async-start(bf16[16,128,1024]{2,1,0:T(8,128)(2,1)} %bitcast.142), calls=%async_computation.6 | async-start | bytes 8388608 | tf_op jit(solution)/shard_map/all_to_all | solution.py:44
